TPU v7x, 512 devices: a whole 4x8x8 slice. The times are simulated.
512 devices in a mesh: dp: 8 (over z_lo, core), row: 8 (over y), col: 8 (over z_hi, x).
Axes of the slice: x: 4, y: 8, z: 8 (z_hi: 2, z_lo: 4; z = z_hi * 4 + z_lo), core: 2. Of those that a mesh axis runs over, the one named last changes fastest.
Arguments:
- inputs: bfloat16 [1536, 4096], P('dp', 'row'), may hold values from -6 to 6
- weight: bfloat16 [4096, 14336], P('row', 'col'), may hold values from -0.09375 to 0.09375
- cotangent: bfloat16 [1536, 14336], P(('dp', 'row'), 'col'), may hold values from -6 to 6
- anchor: bfloat16 [4096, 14336], P(('row', 'dp'), 'col'), may hold values from -0.09375 to 0.09375
- first_moment: float32 [4096, 14336], P(('row', 'dp'), 'col'), may hold values from -0.15625 to 0.15625
- second_moment: float32 [4096, 14336], P(('row', 'dp'), 'col'), may hold values from 1e-06 to 0.0001
Outputs:
- outputs: bfloat16 [1536, 14336], P(('dp', 'row'), 'col')
- input_grad: bfloat16 [1536, 4096], P(('dp', 'col'), 'row')
- new_weight: bfloat16 [4096, 14336], P(('row', 'dp'), 'col')
- new_first: float32 [4096, 14336], P(('row', 'dp'), 'col')
- new_second: float32 [4096, 14336], P(('row', 'dp'), 'col')
All inputs are finite; a program needn't handle non-finite values.
Results may differ from a plain program's by a relative error of at most 0.013.
Values may be sent and summed in bfloat16 or wider, within the bound.
A program may use at most 64 MiB of HBM per device.

v0:
```python
import jax
import jax.numpy as jnp
from jax import lax
from jax.sharding import PartitionSpec as P

beta_one = 0.9
beta_two = 0.999
learn_rate = 0.002
anchor_pull = 0.5
epsilon = 1e-08
step_count = 100.0


def forward_pass(inputs, weight):
    return lax.psum_scatter(
        jnp.dot(inputs, weight, preferred_element_type=jnp.float32).astype(jnp.bfloat16),
        "row",
        scatter_dimension=0,
        tiled=True,
    )


def gather_cotangent(cotangent):
    return lax.all_gather(cotangent, "row", axis=0, tiled=True)


def per_device(inputs, weight, cotangent, anchor, first_moment, second_moment):
    outputs = forward_pass(inputs, weight)
    gathered = gather_cotangent(cotangent)
    input_grad = lax.psum_scatter(
        lax.dot_general(
            gathered, weight, (((1,), (1,)), ((), ())), preferred_element_type=jnp.float32
        ).astype(jnp.bfloat16),
        "col",
        scatter_dimension=0,
        tiled=True,
    )
    slice_rows = weight.shape[0] // lax.axis_size("dp")
    full_grad = lax.dot_general(
        inputs, gathered, (((0,), (0,)), ((), ())), preferred_element_type=jnp.float32
    )
    summed = lax.psum_scatter(
        full_grad.astype(jnp.bfloat16), "dp", scatter_dimension=0, tiled=True
    ).astype(jnp.float32)
    tokens_all = inputs.shape[0] * lax.axis_size("dp")
    own_start = lax.axis_index("dp") * slice_rows
    current = lax.dynamic_slice_in_dim(weight, own_start, slice_rows, 0).astype(jnp.float32)
    grad = summed / tokens_all + anchor_pull * (current - anchor.astype(jnp.float32))
    new_first = beta_one * first_moment + (1.0 - beta_one) * grad
    new_second = beta_two * second_moment + (1.0 - beta_two) * grad * grad
    mhat = new_first / (1.0 - beta_one**step_count)
    vhat = new_second / (1.0 - beta_two**step_count)
    new_weight = (current - learn_rate * mhat / (jnp.sqrt(vhat) + epsilon)).astype(jnp.bfloat16)
    return (outputs, input_grad, new_weight, new_first, new_second)


def solution(mesh):
    in_specs = (
        P("dp", "row"),
        P("row", "col"),
        P(("dp", "row"), "col"),
        P(("row", "dp"), "col"),
        P(("row", "dp"), "col"),
        P(("row", "dp"), "col"),
    )
    out_specs = (
        P(("dp", "row"), "col"),
        P(("dp", "col"), "row"),
        P(("row", "dp"), "col"),
        P(("row", "dp"), "col"),
        P(("row", "dp"), "col"),
    )
    return jax.shard_map(
        per_device, mesh=mesh, in_specs=in_specs, out_specs=out_specs, check_vma=False
    )
```

profile of v0, /device:TPU:1, one launch (start us, length us, event | category | flops | bytes accessed | tf_op | source)
XLA Modules:
  0.0 219.8 jit_solution(13499819245752381363)
XLA Ops:
  7.2 0.0 copy-start
  7.2 0.0 reduce-scatter.8.cloned.1.call-start
  7.2 22.9 %all_gather.3 = bf16[192,1792]{1,0:T(8,128)(2,1)S(1)} all-gather(bf16[24,1792]{1,0:T(8,128)(2,1)} %param.8), channel_id=1, replica_groups=mesh['dp'=8,'row'=8,'col'=8] {'row'}, dimensions={0}, use_global_device_ids=true | all-gather | bytes 774144 | tf_op jit(solution)/shard_map/all_gather | solution.py:24
  30.1 0.0 copy-done
  30.1 0.0 copy-start.1
  30.1 1.9 convolution_convert_fusion
  32.0 0.0 reduce-scatter.8.cloned.1.call-update
  32.0 0.0 reduce-scatter.6.cloned.1.call-start
  32.1 0.0 copy-done.1
  32.1 1.4 convolution_convert_fusion.2
  33.5 0.0 copy-start.2
  33.5 0.0 copy-start.3
  33.5 0.0 copy-start.4
  33.5 0.0 reduce-scatter.6.cloned.1.call-update
  33.6 0.0 reduce-scatter.4.cloned.1.call-start
  33.6 1.4 convolution_convert_fusion.1
  35.0 0.0 reduce-scatter.4.cloned.1.call-update
  35.0 47.0 %reduce-scatter.8.cloned.1.call-done = bf16[64,1792]{1,0:T(8,128)(2,1)} async-done(((bf16[512,1792]{1,0:T(8,128)(2,1)}), bf16[64,1792]{1,0:T(8,128)(2,1)}) %reduce-scatter.8.cloned.1.call-update) | async-done | bytes 229392 | tf_op jit(solution)/shard_map/reduce_scatter | solution.py:42
  82.0 0.0 copy-done.2
  82.0 0.0 copy-done.3
  82.0 0.0 copy-done.4
  82.0 2.2 %fusion.2 = (bf16[64,1792]{1,0:T(8,128)(2,1)}, f32[64,1792]{1,0:T(8,128)}, f32[64,1792]{1,0:T(8,128)}) fusion(bf16[512,1792]{1,0:T(8,128)(2,1)S(1)} %copy-done.1, s32[]{:T(128)S(6)} %select_n.3, bf16[64,1792]{1,0:T(8,128)(2,1)S(1)} %copy-done.4, bf16[64,1792]{1,0:T(8,128)(2,1)} %reduce-scatter.8.cloned.1.call-done, f32[64,1792]{1,0:T(8,128)S(1)} %copy-done.2, ...), kind=kLoop, calls=%fused_computation.8 | loop fusion | flops 2293760 | bytes 2752516 | tf_op jit(solution)/shard_map/convert_element_type | solution.py:53
  84.3 91.8 %reduce-scatter.6.cloned.1.call-done = bf16[24,512]{1,0:T(8,128)(2,1)} async-done(((bf16[192,512]{1,0:T(8,128)(2,1)}), bf16[24,512]{1,0:T(8,128)(2,1)}) %reduce-scatter.6.cloned.1.call-update) | async-done | bytes 24592 | tf_op jit(solution)/shard_map/reduce_scatter | solution.py:30
  176.1 37.2 %reduce-scatter.4.cloned.1.call-done = bf16[24,1792]{1,0:T(8,128)(2,1)} async-done(((bf16[192,1792]{1,0:T(8,128)(2,1)}), bf16[24,1792]{1,0:T(8,128)(2,1)}) %reduce-scatter.4.cloned.1.call-update) | async-done | bytes 86032 | tf_op jit(solution)/shard_map/reduce_scatter | solution.py:15
Async XLA Ops:
  7.2 22.9 %copy-start = (bf16[192,512]{1,0:T(8,128)(2,1)S(1)}, bf16[192,512]{1,0:T(8,128)(2,1)}, u32[]{:S(2)}) copy-start(bf16[192,512]{1,0:T(8,128)(2,1)} %param.6) | copy-start | bytes 589828
  7.2 74.8 %reduce-scatter.8.cloned.1.call-start = ((), (), s32[]{:S(2)}) async-start(), calls=%async_computation.5 | async-start | bytes 2064384 | tf_op jit(solution)/shard_map/reduce_scatter | solution.py:42
  30.1 2.0 copy-start.1
  32.0 144.0 %reduce-scatter.6.cloned.1.call-start = ((), (), s32[]{:S(2)}) async-start(), calls=%async_computation.4 | async-start | bytes 221184 | tf_op jit(solution)/shard_map/reduce_scatter | solution.py:30
  33.5 48.5 %copy-start.2 = (f32[64,1792]{1,0:T(8,128)S(1)}, f32[64,1792]{1,0:T(8,128)}, u32[]{:S(2)}) copy-start(f32[64,1792]{1,0:T(8,128)} %param.10) | copy-start | bytes 1376260
  33.5 48.5 %copy-start.3 = (f32[64,1792]{1,0:T(8,128)S(1)}, f32[64,1792]{1,0:T(8,128)}, u32[]{:S(2)}) copy-start(f32[64,1792]{1,0:T(8,128)} %param.11) | copy-start | bytes 1376260
  33.5 48.5 %copy-start.4 = (bf16[64,1792]{1,0:T(8,128)(2,1)S(1)}, bf16[64,1792]{1,0:T(8,128)(2,1)}, u32[]{:S(2)}) copy-start(bf16[64,1792]{1,0:T(8,128)(2,1)} %param.9) | copy-start | bytes 688132
  33.6 179.7 %reduce-scatter.4.cloned.1.call-start = ((), (), s32[]{:S(2)}) async-start(), calls=%async_computation.3 | async-start | bytes 774144 | tf_op jit(solution)/shard_map/reduce_scatter | solution.py:15
Sparse Core Ops, SparseCore 0:
  32.2 49.8 reduce-scatter.7
  87.0 88.9 reduce-scatter.5
  179.5 33.7 reduce-scatter.3
where the time goes:
time: 224 us; the launch traced here: 220 us
  waiting for transfers between devices  176 us (79%)
  blocking collectives  22.9 us (10%)
  between operations  13.8 us (6%)
  matrix products  4.75 us (2%)
    reduce_scatter x1, waiting for transfers between devices, per_device(): lax.psum_scatter(lax.dot_general(gathered, weight, (((1,), (1,)), ((), ()...  91.8 us
    reduce_scatter x1, waiting for transfers between devices, per_device(): lax.psum_scatter(full_grad.astype(jnp.bfloat16), 'dp', scatter_dimension=...  47 us
    reduce_scatter x1, waiting for transfers between devices, forward_pass(): lax.psum_scatter(jnp.dot(inputs, weight, preferred_element_type=jnp.float...  37.2 us
    all_gather x1, blocking collectives, gather_cotangent(): return lax.all_gather(cotangent, 'row', axis=0, tiled=True)  22.9 us
  transfers between devices with their start and end apart: 3, of which 3 were waited for; matrix products, arithmetic and copies ran while one was open for 2% of the time, Pallas kernels for 0%

commit v1 on v0

v1 whole, which is shorter than its diff:
```python
import functools

import jax
import jax.numpy as jnp
from jax import lax
from jax.experimental import pallas as pl
from jax.experimental.pallas import tpu as pltpu
from jax.sharding import PartitionSpec as P

beta_one = 0.9
beta_two = 0.999
learn_rate = 0.002
anchor_pull = 0.5
epsilon = 1e-08
step_count = 100.0

MESH = pl.DeviceIdType.MESH
f32, bf16 = jnp.float32, jnp.bfloat16
NZ = 4


def chunks_of(width):
    if width == 1792:
        sizes = (256, 512, 512, 512)
    else:
        sizes = (128,) * (width // 128)
    out, at = [], 0
    for size in sizes:
        out.append((at, size))
        at += size
    return out


def kernel(
    n_row, n_x, n_zh, tokens,
    x_ref, w_ref, ct_ref, an_ref, m_ref, v_ref,
    out_ref, ig_ref, nw_ref, nm_ref, nv_ref,
    xv, xpv, wv, ctb, ctp, xts, xs, xps, pb, rsr, gacc, gp, xr, zhs, zhr,
    zs, zr, acc, anv, mv, vv, outv, igv, nwv, nmv, nvv,
    load_sem, store_sem, x_sem, core_send, core_recv, ag_send, ag_recv, rs_send, rs_recv,
    z_send, z_recv, gx_send, gx_recv, zh_sem,
):
    width = w_ref.shape[1]
    T, DR = x_ref.shape
    blocks_of_rows = 2 * NZ
    own = DR // blocks_of_rows
    chunks = chunks_of(width)
    nk = len(chunks)
    dp, r, q = lax.axis_index("dp"), lax.axis_index("row"), lax.axis_index("col")
    z, c = dp // 2, dp % 2
    zh, xx = q // n_x, q % n_x
    right, left = lax.rem(r + 1, n_row), lax.rem(r + n_row - 1, n_row)
    ring = (right, left)
    sign = (1, -1)
    partner = 2 * z + (1 - c)

    def at_row(offset):
        return lax.rem(r + offset + 2 * n_row, n_row)

    def remote(src, dst, ssem, rsem, **device):
        return pltpu.make_async_remote_copy(
            src_ref=src, dst_ref=dst, send_sem=ssem, recv_sem=rsem,
            device_id=device, device_id_type=MESH,
        )

    barrier = pltpu.get_barrier_semaphore()
    greet = [dict(row=right), dict(row=left), dict(dp=partner)]
    for j in range(1, n_x):
        greet.append(dict(col=zh * n_x + lax.rem(xx + j, n_x)))
    if n_zh == 2:
        greet.append(dict(col=(1 - zh) * n_x + xx))
    for device in greet:
        pl.semaphore_signal(barrier, inc=1, device_id=device, device_id_type=MESH)
    for d in range(NZ):
        @pl.when((z != d) & (z + 3 != d) & (z != d + 3))
        def _():
            pl.semaphore_signal(barrier, inc=1, device_id=dict(dp=2 * d + c), device_id_type=MESH)

    loads = [
        pltpu.make_async_copy(x_ref, xv, load_sem.at[0]),
        pltpu.make_async_copy(w_ref, wv, load_sem.at[1]),
        pltpu.make_async_copy(ct_ref, ctb.at[r], load_sem.at[2]),
        pltpu.make_async_copy(m_ref, mv, load_sem.at[3]),
        pltpu.make_async_copy(v_ref, vv, load_sem.at[4]),
        pltpu.make_async_copy(an_ref, anv, load_sem.at[5]),
    ]
    for i in (2, 0, 1, 3, 4, 5):
        loads[i].start()

    def select(src, dst):
        xts[...] = src[...].T.reshape(NZ, 2, own, T)
        dst[...] = xts[:, c].reshape(NZ * own, T)

    loads[0].wait()
    select(xv, xs)
    loads[2].wait()
    pl.semaphore_wait(barrier, len(greet) + 2 + jnp.where((z == 1) | (z == 2), 1, 0))

    sends = []

    def go(copy):
        copy.start()
        sends.append(copy)

    def steps_of(k, d):
        return n_row // 2 if (k + d) % 2 == 0 else (n_row - 1) // 2

    def ag_copy(k, d, hop, receiving):
        cols = pl.ds(chunks[k][0], chunks[k][1])
        block = at_row(-sign[d] * (hop + (1 if receiving else 0)))
        view = ctb.at[block, :, :, cols]
        return remote(view, view, ag_send.at[k, d, hop], ag_recv.at[k, d, hop], row=ring[d])

    def core_copy(k, offset):
        cols = pl.ds(chunks[k][0], chunks[k][1])
        block = at_row(offset)
        slot = offset % n_row
        return remote(
            ctb.at[block, :, :, cols], ctp.at[block, :, :, cols],
            core_send.at[k, slot], core_recv.at[k, slot], dp=partner,
        )

    x_copy = remote(xv, xpv, x_sem.at[0], x_sem.at[1], dp=partner)
    for k in range(nk):
        for d in range(2):
            if steps_of(k, d):
                go(ag_copy(k, d, 0, False))
        if k == 0:
            go(x_copy)
        go(core_copy(k, 0))

    loads[1].wait()
    for at, size in chunks:
        part = jnp.dot(xv[...], wv[:, at:at + size], preferred_element_type=f32)
        pb[:, :, :, at:at + size] = part.reshape(n_row, 3, 8, size).astype(bf16)

    x_copy.wait_recv()
    select(xpv, xps)

    def gather(k):
        for hop in range(n_row // 2):
            for d in range(2):
                if hop < steps_of(k, d):
                    ag_copy(k, d, hop, True).wait_recv()
                    if hop + 1 < steps_of(k, d):
                        go(ag_copy(k, d, hop + 1, False))
                    go(core_copy(k, -sign[d] * (hop + 1)))

    def rows_of(ref, at, size):
        return ref[:, :, :, at:at + size].astype(f32).reshape(T, size).astype(bf16)

    def multiply(k):
        at, size = chunks[k]
        for slot in range(n_row):
            core_copy(k, slot).wait_recv()
        mine = rows_of(ctb, at, size)
        other = rows_of(ctp, at, size)
        grad = jnp.dot(xs[...], mine, preferred_element_type=f32)
        grad = grad + jnp.dot(xps[...], other, preferred_element_type=f32)
        zs[:, :, at:at + size] = grad.reshape(NZ, own, size).astype(bf16)
        return mine

    def input_part(k, mine):
        at, size = chunks[k]
        part = lax.dot_general(
            mine, wv[:, at:at + size], (((1,), (1,)), ((), ())), preferred_element_type=f32
        )
        gacc[...] = part if k == 0 else gacc[...] + part

    def z_copy(k, source, target, slot):
        cols = pl.ds(chunks[k][0], chunks[k][1])
        return remote(
            zs.at[target, :, cols], zr.at[slot, :, cols],
            z_send.at[k, target], z_recv.at[k, slot], dp=2 * source + c,
        )

    def is_relay(d):
        return (z == 1) if d == 3 else (z == 2) if d == 0 else None

    def z_direct(k):
        for d, end, via in ((3, 0, 1), (0, 3, 2)):
            @pl.when(z == end)
            def _():
                z_copy(k, via, d, NZ).start()
        for d in (2, 1, 0, 3):
            ok = z != d
            if d == 3:
                ok = z == 2
            if d == 0:
                ok = z == 1
            @pl.when(ok)
            def _():
                z_copy(k, d, d, z).start()

    def z_relay(k):
        at, size = chunks[k]
        for d, via in ((3, 1), (0, 2)):
            @pl.when(z == via)
            def _():
                z_copy(k, d, d, NZ).wait_recv()
                both = zs[d, :, at:at + size].astype(f32) + zr[NZ, :, at:at + size].astype(f32)
                zs[d, :, at:at + size] = both.astype(bf16)
                z_copy(k, d, d, z).start()

    def z_wait_sends(k):
        for d in range(NZ):
            @pl.when(z != d)
            def _():
                z_copy(k, d, d, 0).wait_send()

    stores = []

    def put(src, dst, sem):
        copy = pltpu.make_async_copy(src, dst, sem)
        copy.start()
        stores.append(copy)

    def update(k):
        at, size = chunks[k]
        cols = pl.ds(at, size)
        acc[:, :size] = zs[z, :, at:at + size].astype(f32)
        for s in range(NZ):
            @pl.when((z != s) & (z + 3 != s) & (z != s + 3))
            def _():
                z_copy(k, s, s, s).wait_recv()
                acc[:, :size] += zr[s, :, at:at + size].astype(f32)
        rows = pl.ds(pl.multiple_of(dp * own, own), own)
        current = wv[rows, at:at + size].astype(f32)
        grad = acc[:, :size] * (1.0 / tokens) + anchor_pull * (current - anv[:, at:at + size].astype(f32))
        first = beta_one * mv[:, at:at + size] + (1.0 - beta_one) * grad
        second = beta_two * vv[:, at:at + size] + (1.0 - beta_two) * grad * grad
        nmv[:, at:at + size] = first
        nvv[:, at:at + size] = second
        put(nmv.at[:, cols], nm_ref.at[:, cols], store_sem.at[k, 0])
        put(nvv.at[:, cols], nv_ref.at[:, cols], store_sem.at[k, 1])
        mhat = first * (1.0 / (1.0 - beta_one**step_count))
        vhat = second * (1.0 / (1.0 - beta_two**step_count))
        nwv[:, at:at + size] = (current - learn_rate * mhat / (jnp.sqrt(vhat) + epsilon)).astype(bf16)
        put(nwv.at[:, cols], nw_ref.at[:, cols], store_sem.at[k, 2])

    half = width // 2

    def rs_copy(h, d, step, receiving):
        total = steps_of(h, d)
        cols = pl.ds(h * half, half)
        target = at_row(sign[d] * (total - step - (1 if receiving else 0)))
        return remote(
            pb.at[target, :, :, cols], rsr.at[d, step, :, :, cols],
            rs_send.at[h, d, step], rs_recv.at[h, d, step], row=ring[d],
        )

    def rs_step(step):
        for h in range(2):
            for d in range(2):
                total = steps_of(h, d)
                cols = slice(h * half, (h + 1) * half)
                if step and step <= total:
                    rs_copy(h, d, step - 1, True).wait_recv()
                    if step < total:
                        block = at_row(sign[d] * (total - step))
                        both = pb[block, :, :, cols].astype(f32) + rsr[d, step - 1, :, :, cols].astype(f32)
                        pb[block, :, :, cols] = both.astype(bf16)
                if step < total:
                    go(rs_copy(h, d, step, False))

    def rs_finish():
        for h in range(2):
            cols = slice(h * half, (h + 1) * half)
            total = pb[r, :, :, cols].astype(f32)
            for d in range(2):
                if steps_of(h, d):
                    total = total + rsr[d, steps_of(h, d) - 1, :, :, cols].astype(f32)
            outv[:, :, cols] = total.astype(bf16)
        put(outv, out_ref, store_sem.at[nk, 0])

    def gx_copy(j):
        target = lax.rem(xx + j, n_x)
        return remote(
            gp.at[:, target], xr.at[j - 1], gx_send.at[j - 1], gx_recv.at[j - 1],
            col=zh * n_x + target,
        )

    def gx_start():
        gp[...] = gacc[...].reshape(n_zh, n_x, 3, 8, DR).astype(bf16)
        for j in range(1, n_x):
            go(gx_copy(j))

    def zh_copy():
        return remote(zhs, zhr, zh_sem.at[0], zh_sem.at[1], col=(1 - zh) * n_x + xx)

    def gx_finish():
        for j in range(1, n_x):
            gx_copy(j).wait_recv()

        def total(side):
            out = gp[side, xx].astype(f32)
            for j in range(1, n_x):
                out = out + xr[j - 1, side].astype(f32)
            return out

        if n_zh == 2:
            zhs[...] = total(1 - zh).astype(bf16)
            go(zh_copy())
        igv[...] = total(zh).astype(bf16)

    def ig_finish():
        if n_zh == 2:
            zh_copy().wait_recv()
            igv[...] = (igv[...].astype(f32) + zhr[...].astype(f32)).astype(bf16)
        put(igv, ig_ref, store_sem.at[nk, 1])

    rs_total = n_row // 2
    rs_next = 0
    for k in range(nk):
        gather(k)
        mine = multiply(k)
        z_direct(k)
        input_part(k, mine)
        if k:
            z_relay(k - 1)
        if k >= nk - 2:
            rs_step(rs_next)
            rs_next += 1
    gx_start()
    rs_step(rs_next)
    rs_next += 1
    z_relay(nk - 1)
    gx_finish()
    for i in (3, 4, 5):
        loads[i].wait()
    update(0)
    while rs_next <= rs_total:
        rs_step(rs_next)
        rs_next += 1
    for k in range(1, nk - 1):
        update(k)
    rs_finish()
    ig_finish()
    update(nk - 1)

    for copy in sends:
        copy.wait_send()
    for k in range(nk):
        z_wait_sends(k)
    for copy in stores:
        copy.wait()


def make_per_device(n_row, n_x, n_zh, n_dp=8):
    def per_device(inputs, weight, cotangent, anchor, first_moment, second_moment):
        T, DR = inputs.shape
        width = weight.shape[1]
        own = DR // n_dp
        nk = len(chunks_of(width))
        hops = max(n_row // 2, 1)
        tall = cotangent.reshape(3, 8, width)
        dma = pltpu.SemaphoreType.DMA
        V = pltpu.VMEM
        scratch = [
            V((T, DR), bf16), V((T, DR), bf16), V((DR, width), bf16),
            V((n_row, 3, 8, width), bf16), V((n_row, 3, 8, width), bf16),
            V((NZ, 2, own, T), bf16), V((NZ * own, T), bf16), V((NZ * own, T), bf16),
            V((n_row, 3, 8, width), bf16), V((2, hops, 3, 8, width), bf16),
            V((T, DR), f32), V((n_zh, n_x, 3, 8, DR), bf16), V((n_x - 1, n_zh, 3, 8, DR), bf16),
            V((3, 8, DR), bf16), V((3, 8, DR), bf16),
            V((NZ, own, width), bf16), V((NZ + 1, own, width), bf16), V((own, 512), f32),
            V((own, width), bf16), V((own, width), f32), V((own, width), f32),
            V((3, 8, width), bf16), V((3, 8, DR), bf16),
            V((own, width), bf16), V((own, width), f32), V((own, width), f32),
            dma((6,)), dma((nk + 1, 3)), dma((2,)),
            dma((nk, n_row)), dma((nk, n_row)),
            dma((nk, 2, hops)), dma((nk, 2, hops)),
            dma((2, 2, hops)), dma((2, 2, hops)),
            dma((nk, NZ)), dma((nk, NZ + 1)),
            dma((n_x - 1,)), dma((n_x - 1,)), dma((2,)),
        ]
        hbm = pl.BlockSpec(memory_space=pl.ANY)
        out, ig, nw, nm, nv = pl.pallas_call(
            functools.partial(kernel, n_row, n_x, n_zh, T * n_dp),
            out_shape=(
                jax.ShapeDtypeStruct((3, 8, width), bf16),
                jax.ShapeDtypeStruct((3, 8, DR), bf16),
                jax.ShapeDtypeStruct((own, width), bf16),
                jax.ShapeDtypeStruct((own, width), f32),
                jax.ShapeDtypeStruct((own, width), f32),
            ),
            in_specs=[hbm] * 6,
            out_specs=(hbm,) * 5,
            scratch_shapes=scratch,
            compiler_params=pltpu.CompilerParams(
                collective_id=0, has_side_effects=True, vmem_limit_bytes=48 * 1024 * 1024
            ),
        )(inputs, weight, tall, anchor, first_moment, second_moment)
        return out.reshape(24, width), ig.reshape(24, DR), nw, nm, nv

    return per_device


def solution(mesh):
    in_specs = (
        P("dp", "row"),
        P("row", "col"),
        P(("dp", "row"), "col"),
        P(("row", "dp"), "col"),
        P(("row", "dp"), "col"),
        P(("row", "dp"), "col"),
    )
    out_specs = (
        P(("dp", "row"), "col"),
        P(("dp", "col"), "row"),
        P(("row", "dp"), "col"),
        P(("row", "dp"), "col"),
        P(("row", "dp"), "col"),
    )
    n_row, n_col = mesh.shape["row"], mesh.shape["col"]
    n_zh = 2 if n_col > 2 else 1
    return jax.shard_map(
        make_per_device(n_row, n_col // n_zh, n_zh), mesh=mesh,
        in_specs=in_specs, out_specs=out_specs, check_vma=False,
    )
```

time: 224 us -> 81.2 us (0.36); the launches traced: 220 us -> 80.9 us
  waiting for transfers between devices: 176 us -> 0 us
  Pallas kernels: 0 us -> 70.5 us
  blocking collectives: 22.9 us -> 0 us
  between operations: 13.8 us -> 0.66 us
  local copies, waits for them, and re-layouts: 0.02 us -> 9.75 us
  matrix products: 4.75 us -> 0 us
    reduce_scatter x3 -> x0, waiting for transfers between devices: 176 us -> none  [the longest x1 91.8 us: per_device(): lax.psum_scatter(lax.dot_general(gathered, weight, (((1,), (1,)), ((), ()...]
    pallas_call x0 -> x1, Pallas kernels: none -> 70.5 us  [per_device(): pl.pallas_call(functools.partial(kernel, n_row, n_x, n_zh, T * n_dp), out...]
    all_gather x1 -> x0, blocking collectives: 22.9 us -> none  [gather_cotangent(): return lax.all_gather(cotangent, 'row', axis=0, tiled=True)]
    unnamed x10 -> x17, local copies, waits for them, and re-layouts: 0.02 us -> 9.75 us
    dot_general x3 -> x0, matrix products: 4.75 us -> none  [the longest x1 1.93 us: per_device(): lax.dot_general(inputs, gathered, (((0,), (0,)), ((), ())), preferred_ele...]
  transfers between devices with their start and end apart: 3 -> 0, of which waited for: 3 -> 0; matrix products, arithmetic and copies ran while one was open for 2% -> 0% of each run, Pallas kernels for 0% -> 0%
where the time goes in v1:
time: 81.2 us; the launch traced here: 80.9 us
  Pallas kernels  70.5 us (87%)
  local copies, waits for them, and re-layouts  9.75 us (12%)
    pallas_call x1, Pallas kernels, per_device(): pl.pallas_call(functools.partial(kernel, n_row, n_x, n_zh, T * n_dp), out...  70.5 us
    unnamed x17, local copies, waits for them, and re-layouts  9.75 us

profile of v1, /device:TPU:1, one launch (start us, length us, event | category | flops | bytes accessed | tf_op | source)
XLA Modules:
  0.0 80.9 jit_solution(2858744477580057343)
XLA Ops:
  0.6 0.0 copy-start
  0.6 1.5 %copy-done = bf16[512,1792]{1,0:T(8,128)(2,1)S(1)} copy-done((bf16[512,1792]{1,0:T(8,128)(2,1)S(1)}, bf16[512,1792]{1,0:T(8,128)(2,1)}, u32[]{:S(2)}) %copy-start) | copy-done | bytes 1835032
  2.1 0.0 copy-start.1
  2.1 1.0 %copy-done.1 = f32[64,1792]{1,0:T(8,128)S(1)} copy-done((f32[64,1792]{1,0:T(8,128)S(1)}, f32[64,1792]{1,0:T(8,128)}, u32[]{:S(2)}) %copy-start.1) | copy-done | bytes 458776
  3.2 0.0 copy-start.2
  3.2 1.0 %copy-done.2 = f32[64,1792]{1,0:T(8,128)S(1)} copy-done((f32[64,1792]{1,0:T(8,128)S(1)}, f32[64,1792]{1,0:T(8,128)}, u32[]{:S(2)}) %copy-start.2) | copy-done | bytes 458776
  4.2 0.0 copy-start.3
  4.2 0.9 %copy-done.3 = bf16[64,1792]{1,0:T(8,128)(2,1)S(1)} copy-done((bf16[64,1792]{1,0:T(8,128)(2,1)S(1)}, bf16[64,1792]{1,0:T(8,128)(2,1)}, u32[]{:S(2)}) %copy-start.3) | copy-done | bytes 229400
  5.1 0.0 copy-start.4
  5.1 0.9 %copy-done.4 = bf16[192,512]{1,0:T(8,128)(2,1)S(1)} copy-done((bf16[192,512]{1,0:T(8,128)(2,1)S(1)}, bf16[192,512]{1,0:T(8,128)(2,1)}, u32[]{:S(2)}) %copy-start.4) | copy-done | bytes 196632
  6.0 0.0 copy-start.5
  6.0 0.9 %copy-done.5 = bf16[24,1792]{1,0:T(8,128)(2,1)S(1)} copy-done((bf16[24,1792]{1,0:T(8,128)(2,1)S(1)}, bf16[24,1792]{1,0:T(8,128)(2,1)}, u32[]{:S(2)}) %copy-start.5) | copy-done | bytes 86040
  6.9 70.5 %shard_map.101 = (bf16[3,8,1792]{2,1,0:T(8,128)(2,1)S(1)}, bf16[3,8,512]{2,1,0:T(8,128)(2,1)S(1)}, bf16[64,1792]{1,0:T(8,128)(2,1)S(1)}, f32[64,1792]{1,0:T(8,128)S(1)}, f32[64,1792]{1,0:T(8,128)S(1)}) custom-call(bf16[192,512]{1,0:T(8,128)(2,1)S(1)} %copy-done.4, bf16[512,1792]{1,0:T(8,128)(2,1)S(1)} %copy-done, bf16[3,8,1792]{2,1,0:T(8,128)(2,1)S(1)} %bitcast.3, ...), custom_call_target="tpu_custom_call" | custom-call | tf_op jit(solution)/shard_map/pallas_call | solution.py:378
  77.4 0.6 copy.16
  78.0 0.6 copy.17
  78.6 0.7 copy.18
  79.3 0.8 copy.19
  80.1 0.8 copy.20
Async XLA Ops:
  0.6 1.5 %copy-start = (bf16[512,1792]{1,0:T(8,128)(2,1)S(1)}, bf16[512,1792]{1,0:T(8,128)(2,1)}, u32[]{:S(2)}) copy-start(bf16[512,1792]{1,0:T(8,128)(2,1)} %w_ref.1) | copy-start | bytes 5505028
  2.1 1.0 %copy-start.1 = (f32[64,1792]{1,0:T(8,128)S(1)}, f32[64,1792]{1,0:T(8,128)}, u32[]{:S(2)}) copy-start(f32[64,1792]{1,0:T(8,128)} %m_ref.1) | copy-start | bytes 1376260
  3.2 1.0 %copy-start.2 = (f32[64,1792]{1,0:T(8,128)S(1)}, f32[64,1792]{1,0:T(8,128)}, u32[]{:S(2)}) copy-start(f32[64,1792]{1,0:T(8,128)} %v_ref.1) | copy-start | bytes 1376260
  4.2 0.9 %copy-start.3 = (bf16[64,1792]{1,0:T(8,128)(2,1)S(1)}, bf16[64,1792]{1,0:T(8,128)(2,1)}, u32[]{:S(2)}) copy-start(bf16[64,1792]{1,0:T(8,128)(2,1)} %an_ref.1) | copy-start | bytes 688132
  5.1 0.9 %copy-start.4 = (bf16[192,512]{1,0:T(8,128)(2,1)S(1)}, bf16[192,512]{1,0:T(8,128)(2,1)}, u32[]{:S(2)}) copy-start(bf16[192,512]{1,0:T(8,128)(2,1)} %x_ref.1) | copy-start | bytes 589828
  6.0 0.9 %copy-start.5 = (bf16[24,1792]{1,0:T(8,128)(2,1)S(1)}, bf16[24,1792]{1,0:T(8,128)(2,1)}, u32[]{:S(2)}) copy-start(bf16[24,1792]{1,0:T(8,128)(2,1)} %param.8) | copy-start | bytes 258052

commit v2 on v1

--- a/solution.py
+++ b/solution.py
@@ -71,10 +71,12 @@
         greet.append(dict(col=(1 - zh) * n_x + xx))
     for device in greet:
         pl.semaphore_signal(barrier, inc=1, device_id=device, device_id_type=MESH)
-    for d in range(NZ):
-        @pl.when((z != d) & (z + 3 != d) & (z != d + 3))
+    for step, inner in ((1, z < NZ - 1), (-1, z > 0)):
+        @pl.when(inner)
         def _():
-            pl.semaphore_signal(barrier, inc=1, device_id=dict(dp=2 * d + c), device_id_type=MESH)
+            pl.semaphore_signal(
+                barrier, inc=1, device_id=dict(dp=2 * (z + step) + c), device_id_type=MESH
+            )
 
     loads = [
         pltpu.make_async_copy(x_ref, xv, load_sem.at[0]),
@@ -94,7 +96,7 @@
     loads[0].wait()
     select(xv, xs)
     loads[2].wait()
-    pl.semaphore_wait(barrier, len(greet) + 2 + jnp.where((z == 1) | (z == 2), 1, 0))
+    pl.semaphore_wait(barrier, len(greet) + 1 + jnp.where((z == 1) | (z == 2), 1, 0))
 
     sends = []
 
@@ -134,17 +136,13 @@
         part = jnp.dot(xv[...], wv[:, at:at + size], preferred_element_type=f32)
         pb[:, :, :, at:at + size] = part.reshape(n_row, 3, 8, size).astype(bf16)
 
-    x_copy.wait_recv()
-    select(xpv, xps)
-
-    def gather(k):
-        for hop in range(n_row // 2):
-            for d in range(2):
-                if hop < steps_of(k, d):
-                    ag_copy(k, d, hop, True).wait_recv()
-                    if hop + 1 < steps_of(k, d):
-                        go(ag_copy(k, d, hop + 1, False))
-                    go(core_copy(k, -sign[d] * (hop + 1)))
+    def gather(k, hop):
+        for d in range(2):
+            if hop < steps_of(k, d):
+                ag_copy(k, d, hop, True).wait_recv()
+                if hop + 1 < steps_of(k, d):
+                    go(ag_copy(k, d, hop + 1, False))
+                go(core_copy(k, -sign[d] * (hop + 1)))
 
     def rows_of(ref, at, size):
         return ref[:, :, :, at:at + size].astype(f32).reshape(T, size).astype(bf16)
@@ -167,46 +165,38 @@
         )
         gacc[...] = part if k == 0 else gacc[...] + part
 
-    def z_copy(k, source, target, slot):
+    def z_copy(k, way, d):
         cols = pl.ds(chunks[k][0], chunks[k][1])
+        to = jnp.minimum(z + 1, NZ - 1) if way == 0 else jnp.maximum(z - 1, 0)
         return remote(
-            zs.at[target, :, cols], zr.at[slot, :, cols],
-            z_send.at[k, target], z_recv.at[k, slot], dp=2 * source + c,
-        )
-
-    def is_relay(d):
-        return (z == 1) if d == 3 else (z == 2) if d == 0 else None
-
-    def z_direct(k):
-        for d, end, via in ((3, 0, 1), (0, 3, 2)):
-            @pl.when(z == end)
+            zs.at[d, :, cols], zr.at[way, d, :, cols],
+            z_send.at[k, d], z_recv.at[way, k, d], dp=2 * to + c,
+        )
+
+    def z_first(k, hops):
+        for way, at_z, d in ((0, 0, hops), (1, NZ - 1, NZ - 1 - hops)):
+            @pl.when(z == at_z)
             def _():
-                z_copy(k, via, d, NZ).start()
-        for d in (2, 1, 0, 3):
-            ok = z != d
-            if d == 3:
-                ok = z == 2
-            if d == 0:
-                ok = z == 1
-            @pl.when(ok)
+                z_copy(k, way, d).start()
+
+    def z_relay(k, at_end, left):
+        at, size = chunks[k]
+        for way in range(2):
+            here = at_end if way == 0 else NZ - 1 - at_end
+            d = here + left if way == 0 else here - left
+
+            @pl.when(z == here)
             def _():
-                z_copy(k, d, d, z).start()
-
-    def z_relay(k):
-        at, size = chunks[k]
-        for d, via in ((3, 1), (0, 2)):
-            @pl.when(z == via)
-            def _():
-                z_copy(k, d, d, NZ).wait_recv()
-                both = zs[d, :, at:at + size].astype(f32) + zr[NZ, :, at:at + size].astype(f32)
+                z_copy(k, way, d).wait_recv()
+                both = zs[d, :, at:at + size].astype(f32) + zr[way, d, :, at:at + size].astype(f32)
                 zs[d, :, at:at + size] = both.astype(bf16)
-                z_copy(k, d, d, z).start()
+                z_copy(k, way, d).start()
 
     def z_wait_sends(k):
         for d in range(NZ):
             @pl.when(z != d)
             def _():
-                z_copy(k, d, d, 0).wait_send()
+                z_copy(k, 0, d).wait_send()
 
     stores = []
 
@@ -219,11 +209,11 @@
         at, size = chunks[k]
         cols = pl.ds(at, size)
         acc[:, :size] = zs[z, :, at:at + size].astype(f32)
-        for s in range(NZ):
-            @pl.when((z != s) & (z + 3 != s) & (z != s + 3))
+        for way, inner in ((0, z > 0), (1, z < NZ - 1)):
+            @pl.when(inner)
             def _():
-                z_copy(k, s, s, s).wait_recv()
-                acc[:, :size] += zr[s, :, at:at + size].astype(f32)
+                z_copy(k, way, z).wait_recv()
+                acc[:, :size] += zr[way, z, :, at:at + size].astype(f32)
         rows = pl.ds(pl.multiple_of(dp * own, own), own)
         current = wv[rows, at:at + size].astype(f32)
         grad = acc[:, :size] * (1.0 / tokens) + anchor_pull * (current - anv[:, at:at + size].astype(f32))
@@ -309,34 +299,50 @@
             igv[...] = (igv[...].astype(f32) + zhr[...].astype(f32)).astype(bf16)
         put(igv, ig_ref, store_sem.at[nk, 1])
 
-    rs_total = n_row // 2
-    rs_next = 0
-    for k in range(nk):
-        gather(k)
+    hops = n_row // 2
+    far = NZ - 1
+
+    def finish_chunk(k):
         mine = multiply(k)
-        z_direct(k)
+        z_first(k, far)
         input_part(k, mine)
+
+    for hop in range(hops):
+        if hop == hops - 1:
+            rs_step(0)
+        for k in range(nk):
+            gather(k, hop)
+            if hop == hops - 1 and k:
+                finish_chunk(k - 1)
+        if hop == 0:
+            x_copy.wait_recv()
+            select(xpv, xps)
+    finish_chunk(nk - 1)
+    gx_start()
+    for k in range(nk):
+        z_first(k, 2)
+    rs_step(1)
+    for k in range(nk + 1):
+        if k < nk:
+            z_relay(k, 1, 2)
+        if k == 2:
+            rs_step(2)
         if k:
-            z_relay(k - 1)
-        if k >= nk - 2:
-            rs_step(rs_next)
-            rs_next += 1
-    gx_start()
-    rs_step(rs_next)
-    rs_next += 1
-    z_relay(nk - 1)
+            z_relay(k - 1, 2, 1)
     gx_finish()
+    for k in range(nk):
+        z_first(k, 1)
+    rs_step(3)
+    for k in range(nk):
+        z_relay(k, 1, 1)
     for i in (3, 4, 5):
         loads[i].wait()
-    update(0)
-    while rs_next <= rs_total:
-        rs_step(rs_next)
-        rs_next += 1
-    for k in range(1, nk - 1):
-        update(k)
+    for step in range(4, hops + 1):
+        rs_step(step)
     rs_finish()
     ig_finish()
-    update(nk - 1)
+    for k in range(nk):
+        update(k)
 
     for copy in sends:
         copy.wait_send()
@@ -344,6 +350,27 @@
         z_wait_sends(k)
     for copy in stores:
         copy.wait()
+
+
+def write_kernel(*refs):
+    n = (len(refs) - 1) // 2
+    copies = [pltpu.make_async_copy(refs[i], refs[n + i], refs[-1].at[i]) for i in range(n)]
+    for copy in copies:
+        copy.start()
+    for copy in copies:
+        copy.wait()
+
+
+def write_out(*arrays):
+    n = len(arrays)
+    return pl.pallas_call(
+        write_kernel,
+        out_shape=tuple(jax.ShapeDtypeStruct(a.shape, a.dtype) for a in arrays),
+        in_specs=[pl.BlockSpec(memory_space=pl.ANY)] * n,
+        out_specs=(pl.BlockSpec(memory_space=pltpu.HBM),) * n,
+        scratch_shapes=[pltpu.SemaphoreType.DMA((n,))],
+        compiler_params=pltpu.CompilerParams(vmem_limit_bytes=4 * 1024 * 1024),
+    )(*arrays)
 
 
 def make_per_device(n_row, n_x, n_zh, n_dp=8):
@@ -363,7 +390,7 @@
             V((n_row, 3, 8, width), bf16), V((2, hops, 3, 8, width), bf16),
             V((T, DR), f32), V((n_zh, n_x, 3, 8, DR), bf16), V((n_x - 1, n_zh, 3, 8, DR), bf16),
             V((3, 8, DR), bf16), V((3, 8, DR), bf16),
-            V((NZ, own, width), bf16), V((NZ + 1, own, width), bf16), V((own, 512), f32),
+            V((NZ, own, width), bf16), V((2, NZ, own, width), bf16), V((own, 512), f32),
             V((own, width), bf16), V((own, width), f32), V((own, width), f32),
             V((3, 8, width), bf16), V((3, 8, DR), bf16),
             V((own, width), bf16), V((own, width), f32), V((own, width), f32),
@@ -371,11 +398,12 @@
             dma((nk, n_row)), dma((nk, n_row)),
             dma((nk, 2, hops)), dma((nk, 2, hops)),
             dma((2, 2, hops)), dma((2, 2, hops)),
-            dma((nk, NZ)), dma((nk, NZ + 1)),
+            dma((nk, NZ)), dma((2, nk, NZ)),
             dma((n_x - 1,)), dma((n_x - 1,)), dma((2,)),
         ]
-        hbm = pl.BlockSpec(memory_space=pl.ANY)
-        out, ig, nw, nm, nv = pl.pallas_call(
+        hbm = pl.BlockSpec(memory_space=pltpu.HBM)
+        anywhere = pl.BlockSpec(memory_space=pl.ANY)
+        results = pl.pallas_call(
             functools.partial(kernel, n_row, n_x, n_zh, T * n_dp),
             out_shape=(
                 jax.ShapeDtypeStruct((3, 8, width), bf16),
@@ -385,13 +413,13 @@
                 jax.ShapeDtypeStruct((own, width), f32),
             ),
             in_specs=[hbm] * 6,
-            out_specs=(hbm,) * 5,
+            out_specs=(anywhere,) * 5,
             scratch_shapes=scratch,
             compiler_params=pltpu.CompilerParams(
                 collective_id=0, has_side_effects=True, vmem_limit_bytes=48 * 1024 * 1024
             ),
-        )(inputs, weight, tall, anchor, first_moment, second_moment)
-        return out.reshape(24, width), ig.reshape(24, DR), nw, nm, nv
+        )(*(pltpu.with_memory_space_constraint(a, pltpu.HBM) for a in (inputs, weight, tall, anchor, first_moment, second_moment)))
+        return write_out(results[0].reshape(24, width), results[1].reshape(24, DR), *results[2:])
 
     return per_device
 

time: 81.2 us -> 47.6 us (0.59)
  the two profiles are of different devices: /device:TPU:1 before, /device:TPU:70 now
where the time goes in v2:
time: 47.6 us; the launch traced here: 47.5 us
  Pallas kernels  46.8 us (98%)
  between operations  0.64 us (1%)
    pallas_call x1, Pallas kernels, per_device(): pl.pallas_call(functools.partial(kernel, n_row, n_x, n_zh, T * n_dp), out...  45.7 us
    pallas_call x1, Pallas kernels, write_out(): pl.pallas_call(write_kernel, out_shape=tuple((jax.ShapeDtypeStruct(a.shap...  1.08 us

profile of v2, /device:TPU:70, one launch (start us, length us, event | category | flops | bytes accessed | tf_op | source)
XLA Modules:
  0.0 47.5 jit_solution(17523443526562111971)
XLA Ops:
  0.6 45.7 %shard_map.101 = (bf16[3,8,1792]{2,1,0:T(8,128)(2,1)S(1)}, bf16[3,8,512]{2,1,0:T(8,128)(2,1)S(1)}, bf16[64,1792]{1,0:T(8,128)(2,1)S(1)}, f32[64,1792]{1,0:T(8,128)S(1)}, f32[64,1792]{1,0:T(8,128)S(1)}) custom-call(bf16[192,512]{1,0:T(8,128)(2,1)} %x_ref.1, bf16[512,1792]{1,0:T(8,128)(2,1)} %w_ref.1, bf16[3,8,1792]{2,1,0:T(8,128)(2,1)} %bitcast.5, ...), custom_call_target="tpu_custom_call" | custom-call | tf_op jit(solution)/shard_map/pallas_call | solution.py:406
  46.4 1.1 %shard_map.102 = (bf16[24,1792]{1,0:T(8,128)(2,1)}, bf16[24,512]{1,0:T(8,128)(2,1)}, bf16[64,1792]{1,0:T(8,128)(2,1)}, f32[64,1792]{1,0:T(8,128)}, f32[64,1792]{1,0:T(8,128)}) custom-call(bf16[24,1792]{1,0:T(8,128)(2,1)S(1)} %bitcast.3, bf16[24,512]{1,0:T(8,128)(2,1)S(1)} %bitcast.4, bf16[64,1792]{1,0:T(8,128)(2,1)S(1)} %get-tuple-element.12.refs_2_, ...), custom_call_target="tpu_custom_call" | custom-call | tf_op jit(solution)/shard_map/pallas_call | solution.py:366

commit v3 on v2

--- a/solution.py
+++ b/solution.py
@@ -21,7 +21,7 @@
 
 def chunks_of(width):
     if width == 1792:
-        sizes = (256, 512, 512, 512)
+        sizes = (512, 384, 512, 384)
     else:
         sizes = (128,) * (width // 128)
     out, at = [], 0
@@ -38,7 +38,7 @@
     xv, xpv, wv, ctb, ctp, xts, xs, xps, pb, rsr, gacc, gp, xr, zhs, zhr,
     zs, zr, acc, anv, mv, vv, outv, igv, nwv, nmv, nvv,
     load_sem, store_sem, x_sem, core_send, core_recv, ag_send, ag_recv, rs_send, rs_recv,
-    z_send, z_recv, gx_send, gx_recv, zh_sem,
+    z_send, z_recv, gx_send, gx_recv, zh_sem, token,
 ):
     width = w_ref.shape[1]
     T, DR = x_ref.shape
@@ -63,20 +63,23 @@
             device_id=device, device_id_type=MESH,
         )
 
+    def along_z(step):
+        at = lax.rem(zh * NZ + z + step + NZ * n_zh, NZ * n_zh)
+        return dict(dp=2 * lax.rem(at, NZ) + c, col=lax.div(at, NZ) * n_x + xx)
+
+    def along_x(step):
+        return dict(col=zh * n_x + lax.rem(xx + step + n_x, n_x))
+
+    def signal(sem, device):
+        pl.semaphore_signal(sem, inc=1, device_id=device, device_id_type=MESH)
+
     barrier = pltpu.get_barrier_semaphore()
-    greet = [dict(row=right), dict(row=left), dict(dp=partner)]
-    for j in range(1, n_x):
-        greet.append(dict(col=zh * n_x + lax.rem(xx + j, n_x)))
-    if n_zh == 2:
-        greet.append(dict(col=(1 - zh) * n_x + xx))
+    greet = [dict(row=right), dict(row=left), dict(dp=partner), along_z(1), along_z(-1)]
+    greet += [along_x(1), along_x(-1)]
+    if n_row > 4:
+        greet += [dict(row=at_row(2)), dict(row=at_row(-2))]
     for device in greet:
-        pl.semaphore_signal(barrier, inc=1, device_id=device, device_id_type=MESH)
-    for step, inner in ((1, z < NZ - 1), (-1, z > 0)):
-        @pl.when(inner)
-        def _():
-            pl.semaphore_signal(
-                barrier, inc=1, device_id=dict(dp=2 * (z + step) + c), device_id_type=MESH
-            )
+        signal(barrier, device)
 
     loads = [
         pltpu.make_async_copy(x_ref, xv, load_sem.at[0]),
@@ -93,10 +96,8 @@
         xts[...] = src[...].T.reshape(NZ, 2, own, T)
         dst[...] = xts[:, c].reshape(NZ * own, T)
 
-    loads[0].wait()
-    select(xv, xs)
     loads[2].wait()
-    pl.semaphore_wait(barrier, len(greet) + 1 + jnp.where((z == 1) | (z == 2), 1, 0))
+    pl.semaphore_wait(barrier, len(greet))
 
     sends = []
 
@@ -104,17 +105,24 @@
         copy.start()
         sends.append(copy)
 
+    pieces = 2
+    piece = width // pieces
+
     def steps_of(k, d):
         return n_row // 2 if (k + d) % 2 == 0 else (n_row - 1) // 2
 
-    def ag_copy(k, d, hop, receiving):
-        cols = pl.ds(chunks[k][0], chunks[k][1])
-        block = at_row(-sign[d] * (hop + (1 if receiving else 0)))
+    def ag_copy(k, d, reach, receiving):
+        cols = pl.ds(k * piece, piece)
+        hops = 1 if reach == 3 else min(reach, 2)
+        block = at_row(-sign[d] * (reach if receiving else reach - hops))
         view = ctb.at[block, :, :, cols]
-        return remote(view, view, ag_send.at[k, d, hop], ag_recv.at[k, d, hop], row=ring[d])
+        return remote(
+            view, view, ag_send.at[k, d, reach - 1], ag_recv.at[k, d, reach - 1],
+            row=at_row(sign[d] * hops),
+        )
 
     def core_copy(k, offset):
-        cols = pl.ds(chunks[k][0], chunks[k][1])
+        cols = pl.ds(k * piece, piece)
         block = at_row(offset)
         slot = offset % n_row
         return remote(
@@ -122,35 +130,46 @@
             core_send.at[k, slot], core_recv.at[k, slot], dp=partner,
         )
 
+    for reach in (2, 1):
+        for k in range(pieces):
+            for d in range(2):
+                if reach <= steps_of(k, d):
+                    go(ag_copy(k, d, reach, False))
+    for k in range(pieces):
+        go(core_copy(k, 0))
+    if n_zh == 2:
+        signal(token.at[0], along_z(1))
+    if n_x > 2:
+        signal(token.at[3], along_x(1))
+    loads[0].wait()
     x_copy = remote(xv, xpv, x_sem.at[0], x_sem.at[1], dp=partner)
-    for k in range(nk):
-        for d in range(2):
-            if steps_of(k, d):
-                go(ag_copy(k, d, 0, False))
-        if k == 0:
-            go(x_copy)
-        go(core_copy(k, 0))
+    go(x_copy)
+    select(xv, xs)
+    if n_zh == 2:
+        pl.semaphore_wait(token.at[0], 1)
+        signal(token.at[1], along_z(1))
 
     loads[1].wait()
     for at, size in chunks:
         part = jnp.dot(xv[...], wv[:, at:at + size], preferred_element_type=f32)
         pb[:, :, :, at:at + size] = part.reshape(n_row, 3, 8, size).astype(bf16)
 
-    def gather(k, hop):
-        for d in range(2):
-            if hop < steps_of(k, d):
-                ag_copy(k, d, hop, True).wait_recv()
-                if hop + 1 < steps_of(k, d):
-                    go(ag_copy(k, d, hop + 1, False))
-                go(core_copy(k, -sign[d] * (hop + 1)))
+    def gather(reach):
+        for k in range(pieces):
+            for d in range(2):
+                if reach <= steps_of(k, d):
+                    ag_copy(k, d, reach, True).wait_recv()
+                    if reach == 2:
+                        for further in (3, 4):
+                            if further <= steps_of(k, d):
+                                go(ag_copy(k, d, further, False))
+                    go(core_copy(k, -sign[d] * reach))
 
     def rows_of(ref, at, size):
         return ref[:, :, :, at:at + size].astype(f32).reshape(T, size).astype(bf16)
 
     def multiply(k):
         at, size = chunks[k]
-        for slot in range(n_row):
-            core_copy(k, slot).wait_recv()
         mine = rows_of(ctb, at, size)
         other = rows_of(ctp, at, size)
         grad = jnp.dot(xs[...], mine, preferred_element_type=f32)
@@ -289,6 +308,7 @@
             return out
 
         if n_zh == 2:
+            pl.semaphore_wait(token.at[2], 1)
             zhs[...] = total(1 - zh).astype(bf16)
             go(zh_copy())
         igv[...] = total(zh).astype(bf16)
@@ -307,17 +327,24 @@
         z_first(k, far)
         input_part(k, mine)
 
-    for hop in range(hops):
-        if hop == hops - 1:
+    reaches = range(1, hops + 1)
+    for reach in sorted(reaches, key=lambda n: abs(n - 2) + n / 8):
+        gather(reach)
+        if reach == min(2, hops):
             rs_step(0)
-        for k in range(nk):
-            gather(k, hop)
-            if hop == hops - 1 and k:
-                finish_chunk(k - 1)
-        if hop == 0:
             x_copy.wait_recv()
             select(xpv, xps)
-    finish_chunk(nk - 1)
+            if n_zh == 2:
+                pl.semaphore_wait(token.at[1], 1)
+                signal(token.at[2], along_z(1))
+    for k in range(pieces):
+        for slot in range(n_row):
+            core_copy(k, slot).wait_recv()
+        for m in range(nk):
+            if k * piece <= chunks[m][0] < (k + 1) * piece:
+                finish_chunk(m)
+    if n_x > 2:
+        pl.semaphore_wait(token.at[3], 1)
     gx_start()
     for k in range(nk):
         z_first(k, 2)
@@ -395,11 +422,12 @@
             V((3, 8, width), bf16), V((3, 8, DR), bf16),
             V((own, width), bf16), V((own, width), f32), V((own, width), f32),
             dma((6,)), dma((nk + 1, 3)), dma((2,)),
-            dma((nk, n_row)), dma((nk, n_row)),
-            dma((nk, 2, hops)), dma((nk, 2, hops)),
+            dma((2, n_row)), dma((2, n_row)),
+            dma((2, 2, hops)), dma((2, 2, hops)),
             dma((2, 2, hops)), dma((2, 2, hops)),
             dma((nk, NZ)), dma((2, nk, NZ)),
             dma((n_x - 1,)), dma((n_x - 1,)), dma((2,)),
+            pltpu.SemaphoreType.REGULAR((4,)),
         ]
         hbm = pl.BlockSpec(memory_space=pltpu.HBM)
         anywhere = pl.BlockSpec(memory_space=pl.ANY)

time: 47.6 us -> 46.4 us (0.975)
  the two profiles are of different devices: /device:TPU:70 before, /device:TPU:64 now
where the time goes in v3:
time: 46.4 us; the launch traced here: 46.3 us
  Pallas kernels  45.6 us (98%)
  between operations  0.64 us (1%)
    pallas_call x1, Pallas kernels, per_device(): pl.pallas_call(functools.partial(kernel, n_row, n_x, n_zh, T * n_dp), out...  44.5 us
    pallas_call x1, Pallas kernels, write_out(): pl.pallas_call(write_kernel, out_shape=tuple((jax.ShapeDtypeStruct(a.shap...  1.08 us

profile of v3, /device:TPU:64, one launch (start us, length us, event | category | flops | bytes accessed | tf_op | source)
XLA Modules:
  0.0 46.3 jit_solution(13090224270406480742)
XLA Ops:
  0.6 44.5 %shard_map.101 = (bf16[3,8,1792]{2,1,0:T(8,128)(2,1)S(1)}, bf16[3,8,512]{2,1,0:T(8,128)(2,1)S(1)}, bf16[64,1792]{1,0:T(8,128)(2,1)S(1)}, f32[64,1792]{1,0:T(8,128)S(1)}, f32[64,1792]{1,0:T(8,128)S(1)}) custom-call(bf16[192,512]{1,0:T(8,128)(2,1)} %x_ref.1, bf16[512,1792]{1,0:T(8,128)(2,1)} %w_ref.1, bf16[3,8,1792]{2,1,0:T(8,128)(2,1)} %bitcast.5, ...), custom_call_target="tpu_custom_call" | custom-call | tf_op jit(solution)/shard_map/pallas_call | solution.py:434
  45.2 1.1 %shard_map.102 = (bf16[24,1792]{1,0:T(8,128)(2,1)}, bf16[24,512]{1,0:T(8,128)(2,1)}, bf16[64,1792]{1,0:T(8,128)(2,1)}, f32[64,1792]{1,0:T(8,128)}, f32[64,1792]{1,0:T(8,128)}) custom-call(bf16[24,1792]{1,0:T(8,128)(2,1)S(1)} %bitcast.3, bf16[24,512]{1,0:T(8,128)(2,1)S(1)} %bitcast.4, bf16[64,1792]{1,0:T(8,128)(2,1)S(1)} %get-tuple-element.12.refs_2_, ...), custom_call_target="tpu_custom_call" | custom-call | tf_op jit(solution)/shard_map/pallas_call | solution.py:393

commit v4 on v3

--- a/solution.py
+++ b/solution.py
@@ -21,7 +21,7 @@
 
 def chunks_of(width):
     if width == 1792:
-        sizes = (512, 384, 512, 384)
+        sizes = (256, 512, 512, 512)
     else:
         sizes = (128,) * (width // 128)
     out, at = [], 0
@@ -35,7 +35,7 @@
     n_row, n_x, n_zh, tokens,
     x_ref, w_ref, ct_ref, an_ref, m_ref, v_ref,
     out_ref, ig_ref, nw_ref, nm_ref, nv_ref,
-    xv, xpv, wv, ctb, ctp, xts, xs, xps, pb, rsr, gacc, gp, xr, zhs, zhr,
+    xv, xpv, wv, ctb, ctp, xts, xs, xps, wacc, pb, rsr, gacc, gp, xr, zhs, zhr,
     zs, zr, acc, anv, mv, vv, outv, igv, nwv, nmv, nvv,
     load_sem, store_sem, x_sem, core_send, core_recv, ag_send, ag_recv, rs_send, rs_recv,
     z_send, z_recv, gx_send, gx_recv, zh_sem, token,
@@ -105,14 +105,11 @@
         copy.start()
         sends.append(copy)
 
-    pieces = 2
-    piece = width // pieces
-
     def steps_of(k, d):
         return n_row // 2 if (k + d) % 2 == 0 else (n_row - 1) // 2
 
     def ag_copy(k, d, reach, receiving):
-        cols = pl.ds(k * piece, piece)
+        cols = pl.ds(chunks[k][0], chunks[k][1])
         hops = 1 if reach == 3 else min(reach, 2)
         block = at_row(-sign[d] * (reach if receiving else reach - hops))
         view = ctb.at[block, :, :, cols]
@@ -122,7 +119,7 @@
         )
 
     def core_copy(k, offset):
-        cols = pl.ds(k * piece, piece)
+        cols = pl.ds(chunks[k][0], chunks[k][1])
         block = at_row(offset)
         slot = offset % n_row
         return remote(
@@ -130,12 +127,12 @@
             core_send.at[k, slot], core_recv.at[k, slot], dp=partner,
         )
 
-    for reach in (2, 1):
-        for k in range(pieces):
+    for k in range(nk):
+        for reach in (2, 1):
             for d in range(2):
                 if reach <= steps_of(k, d):
                     go(ag_copy(k, d, reach, False))
-    for k in range(pieces):
+    for k in range(nk):
         go(core_copy(k, 0))
     if n_zh == 2:
         signal(token.at[0], along_z(1))
@@ -154,35 +151,33 @@
         part = jnp.dot(xv[...], wv[:, at:at + size], preferred_element_type=f32)
         pb[:, :, :, at:at + size] = part.reshape(n_row, 3, 8, size).astype(bf16)
 
-    def gather(reach):
-        for k in range(pieces):
-            for d in range(2):
-                if reach <= steps_of(k, d):
-                    ag_copy(k, d, reach, True).wait_recv()
-                    if reach == 2:
-                        for further in (3, 4):
-                            if further <= steps_of(k, d):
-                                go(ag_copy(k, d, further, False))
-                    go(core_copy(k, -sign[d] * reach))
+    def gather(k, reach):
+        for d in range(2):
+            if reach <= steps_of(k, d):
+                ag_copy(k, d, reach, True).wait_recv()
+                if reach == 2:
+                    for further in (3, 4):
+                        if further <= steps_of(k, d):
+                            go(ag_copy(k, d, further, False))
+                go(core_copy(k, -sign[d] * reach))
 
     def rows_of(ref, at, size):
         return ref[:, :, :, at:at + size].astype(f32).reshape(T, size).astype(bf16)
 
-    def multiply(k):
+    def own_part(k):
         at, size = chunks[k]
         mine = rows_of(ctb, at, size)
-        other = rows_of(ctp, at, size)
-        grad = jnp.dot(xs[...], mine, preferred_element_type=f32)
-        grad = grad + jnp.dot(xps[...], other, preferred_element_type=f32)
-        zs[:, :, at:at + size] = grad.reshape(NZ, own, size).astype(bf16)
-        return mine
-
-    def input_part(k, mine):
-        at, size = chunks[k]
+        wacc[:, at:at + size] = jnp.dot(xs[...], mine, preferred_element_type=f32)
         part = lax.dot_general(
             mine, wv[:, at:at + size], (((1,), (1,)), ((), ())), preferred_element_type=f32
         )
         gacc[...] = part if k == 0 else gacc[...] + part
+
+    def other_part(k):
+        at, size = chunks[k]
+        other = rows_of(ctp, at, size)
+        grad = wacc[:, at:at + size] + jnp.dot(xps[...], other, preferred_element_type=f32)
+        zs[:, :, at:at + size] = grad.reshape(NZ, own, size).astype(bf16)
 
     def z_copy(k, way, d):
         cols = pl.ds(chunks[k][0], chunks[k][1])
@@ -323,43 +318,46 @@
     far = NZ - 1
 
     def finish_chunk(k):
-        mine = multiply(k)
-        z_first(k, far)
-        input_part(k, mine)
-
-    reaches = range(1, hops + 1)
-    for reach in sorted(reaches, key=lambda n: abs(n - 2) + n / 8):
-        gather(reach)
-        if reach == min(2, hops):
-            rs_step(0)
-            x_copy.wait_recv()
-            select(xpv, xps)
-            if n_zh == 2:
-                pl.semaphore_wait(token.at[1], 1)
-                signal(token.at[2], along_z(1))
-    for k in range(pieces):
         for slot in range(n_row):
             core_copy(k, slot).wait_recv()
-        for m in range(nk):
-            if k * piece <= chunks[m][0] < (k + 1) * piece:
-                finish_chunk(m)
+        other_part(k)
+        z_first(k, far)
+
+    for k in range(nk):
+        gather(k, 2)
+    rs_step(0)
+    x_copy.wait_recv()
+    select(xpv, xps)
+    if n_zh == 2:
+        pl.semaphore_wait(token.at[1], 1)
+        signal(token.at[2], along_z(1))
+    for k in range(nk):
+        for reach in range(1, hops + 1):
+            if reach != 2:
+                gather(k, reach)
+        if k:
+            finish_chunk(k - 1)
+        own_part(k)
     if n_x > 2:
         pl.semaphore_wait(token.at[3], 1)
     gx_start()
+    rs_step(1)
+    finish_chunk(nk - 1)
     for k in range(nk):
         z_first(k, 2)
-    rs_step(1)
     for k in range(nk + 1):
         if k < nk:
             z_relay(k, 1, 2)
-        if k == 2:
+        if k == 0:
             rs_step(2)
+        if k == 1:
+            gx_finish()
+        if k == 3:
+            rs_step(3)
         if k:
             z_relay(k - 1, 2, 1)
-    gx_finish()
     for k in range(nk):
         z_first(k, 1)
-    rs_step(3)
     for k in range(nk):
         z_relay(k, 1, 1)
     for i in (3, 4, 5):
@@ -414,6 +412,7 @@
             V((T, DR), bf16), V((T, DR), bf16), V((DR, width), bf16),
             V((n_row, 3, 8, width), bf16), V((n_row, 3, 8, width), bf16),
             V((NZ, 2, own, T), bf16), V((NZ * own, T), bf16), V((NZ * own, T), bf16),
+            V((NZ * own, width), f32),
             V((n_row, 3, 8, width), bf16), V((2, hops, 3, 8, width), bf16),
             V((T, DR), f32), V((n_zh, n_x, 3, 8, DR), bf16), V((n_x - 1, n_zh, 3, 8, DR), bf16),
             V((3, 8, DR), bf16), V((3, 8, DR), bf16),
@@ -422,8 +421,8 @@
             V((3, 8, width), bf16), V((3, 8, DR), bf16),
             V((own, width), bf16), V((own, width), f32), V((own, width), f32),
             dma((6,)), dma((nk + 1, 3)), dma((2,)),
-            dma((2, n_row)), dma((2, n_row)),
-            dma((2, 2, hops)), dma((2, 2, hops)),
+            dma((nk, n_row)), dma((nk, n_row)),
+            dma((nk, 2, hops)), dma((nk, 2, hops)),
             dma((2, 2, hops)), dma((2, 2, hops)),
             dma((nk, NZ)), dma((2, nk, NZ)),
             dma((n_x - 1,)), dma((n_x - 1,)), dma((2,)),

time: 46.4 us -> 44.2 us (0.953)
  the two profiles are of different devices: /device:TPU:64 before, /device:TPU:1 now
where the time goes in v4:
time: 44.2 us; the launch traced here: 44.1 us
  Pallas kernels  43.5 us (98%)
  between operations  0.64 us (1%)
    pallas_call x1, Pallas kernels, per_device(): pl.pallas_call(functools.partial(kernel, n_row, n_x, n_zh, T * n_dp), out...  42.4 us
    pallas_call x1, Pallas kernels, write_out(): pl.pallas_call(write_kernel, out_shape=tuple((jax.ShapeDtypeStruct(a.shap...  1.08 us

profile of v4, /device:TPU:1, one launch (start us, length us, event | category | flops | bytes accessed | tf_op | source)
XLA Modules:
  0.0 44.1 jit_solution(178144587869611824)
XLA Ops:
  0.6 42.4 %shard_map.101 = (bf16[3,8,1792]{2,1,0:T(8,128)(2,1)S(1)}, bf16[3,8,512]{2,1,0:T(8,128)(2,1)S(1)}, bf16[64,1792]{1,0:T(8,128)(2,1)S(1)}, f32[64,1792]{1,0:T(8,128)S(1)}, f32[64,1792]{1,0:T(8,128)S(1)}) custom-call(bf16[192,512]{1,0:T(8,128)(2,1)} %x_ref.1, bf16[512,1792]{1,0:T(8,128)(2,1)} %w_ref.1, bf16[3,8,1792]{2,1,0:T(8,128)(2,1)} %bitcast.5, ...), custom_call_target="tpu_custom_call" | custom-call | tf_op jit(solution)/shard_map/pallas_call | solution.py:433
  43.0 1.1 %shard_map.102 = (bf16[24,1792]{1,0:T(8,128)(2,1)}, bf16[24,512]{1,0:T(8,128)(2,1)}, bf16[64,1792]{1,0:T(8,128)(2,1)}, f32[64,1792]{1,0:T(8,128)}, f32[64,1792]{1,0:T(8,128)}) custom-call(bf16[24,1792]{1,0:T(8,128)(2,1)S(1)} %bitcast.3, bf16[24,512]{1,0:T(8,128)(2,1)S(1)} %bitcast.4, bf16[64,1792]{1,0:T(8,128)(2,1)S(1)} %get-tuple-element.12.refs_2_, ...), custom_call_target="tpu_custom_call" | custom-call | tf_op jit(solution)/shard_map/pallas_call | solution.py:391

commit v5 on v4

--- a/solution.py
+++ b/solution.py
@@ -34,10 +34,10 @@
 def kernel(
     n_row, n_x, n_zh, tokens,
     x_ref, w_ref, ct_ref, an_ref, m_ref, v_ref,
-    out_ref, ig_ref, nw_ref, nm_ref, nv_ref,
+    outv, igv, nwv, nmv, nvv,
     xv, xpv, wv, ctb, ctp, xts, xs, xps, wacc, pb, rsr, gacc, gp, xr, zhs, zhr,
-    zs, zr, acc, anv, mv, vv, outv, igv, nwv, nmv, nvv,
-    load_sem, store_sem, x_sem, core_send, core_recv, ag_send, ag_recv, rs_send, rs_recv,
+    zs, zr, acc, anv, mv, vv,
+    load_sem, x_sem, core_send, core_recv, ag_send, ag_recv, rs_send, rs_recv,
     z_send, z_recv, gx_send, gx_recv, zh_sem, token,
 ):
     width = w_ref.shape[1]
@@ -212,16 +212,8 @@
             def _():
                 z_copy(k, 0, d).wait_send()
 
-    stores = []
-
-    def put(src, dst, sem):
-        copy = pltpu.make_async_copy(src, dst, sem)
-        copy.start()
-        stores.append(copy)
-
     def update(k):
         at, size = chunks[k]
-        cols = pl.ds(at, size)
         acc[:, :size] = zs[z, :, at:at + size].astype(f32)
         for way, inner in ((0, z > 0), (1, z < NZ - 1)):
             @pl.when(inner)
@@ -235,12 +227,9 @@
         second = beta_two * vv[:, at:at + size] + (1.0 - beta_two) * grad * grad
         nmv[:, at:at + size] = first
         nvv[:, at:at + size] = second
-        put(nmv.at[:, cols], nm_ref.at[:, cols], store_sem.at[k, 0])
-        put(nvv.at[:, cols], nv_ref.at[:, cols], store_sem.at[k, 1])
         mhat = first * (1.0 / (1.0 - beta_one**step_count))
         vhat = second * (1.0 / (1.0 - beta_two**step_count))
         nwv[:, at:at + size] = (current - learn_rate * mhat / (jnp.sqrt(vhat) + epsilon)).astype(bf16)
-        put(nwv.at[:, cols], nw_ref.at[:, cols], store_sem.at[k, 2])
 
     half = width // 2
 
@@ -275,7 +264,6 @@
                 if steps_of(h, d):
                     total = total + rsr[d, steps_of(h, d) - 1, :, :, cols].astype(f32)
             outv[:, :, cols] = total.astype(bf16)
-        put(outv, out_ref, store_sem.at[nk, 0])
 
     def gx_copy(j):
         target = lax.rem(xx + j, n_x)
@@ -312,7 +300,6 @@
         if n_zh == 2:
             zh_copy().wait_recv()
             igv[...] = (igv[...].astype(f32) + zhr[...].astype(f32)).astype(bf16)
-        put(igv, ig_ref, store_sem.at[nk, 1])
 
     hops = n_row // 2
     far = NZ - 1
@@ -335,13 +322,14 @@
         for reach in range(1, hops + 1):
             if reach != 2:
                 gather(k, reach)
+        if k == nk - 1:
+            rs_step(1)
         if k:
             finish_chunk(k - 1)
         own_part(k)
     if n_x > 2:
         pl.semaphore_wait(token.at[3], 1)
     gx_start()
-    rs_step(1)
     finish_chunk(nk - 1)
     for k in range(nk):
         z_first(k, 2)
@@ -352,7 +340,7 @@
             rs_step(2)
         if k == 1:
             gx_finish()
-        if k == 3:
+        if k == 2:
             rs_step(3)
         if k:
             z_relay(k - 1, 2, 1)
@@ -373,8 +361,6 @@
         copy.wait_send()
     for k in range(nk):
         z_wait_sends(k)
-    for copy in stores:
-        copy.wait()
 
 
 def write_kernel(*refs):
@@ -418,9 +404,7 @@
             V((3, 8, DR), bf16), V((3, 8, DR), bf16),
             V((NZ, own, width), bf16), V((2, NZ, own, width), bf16), V((own, 512), f32),
             V((own, width), bf16), V((own, width), f32), V((own, width), f32),
-            V((3, 8, width), bf16), V((3, 8, DR), bf16),
-            V((own, width), bf16), V((own, width), f32), V((own, width), f32),
-            dma((6,)), dma((nk + 1, 3)), dma((2,)),
+            dma((6,)), dma((2,)),
             dma((nk, n_row)), dma((nk, n_row)),
             dma((nk, 2, hops)), dma((nk, 2, hops)),
             dma((2, 2, hops)), dma((2, 2, hops)),
@@ -429,7 +413,6 @@
             pltpu.SemaphoreType.REGULAR((4,)),
         ]
         hbm = pl.BlockSpec(memory_space=pltpu.HBM)
-        anywhere = pl.BlockSpec(memory_space=pl.ANY)
         results = pl.pallas_call(
             functools.partial(kernel, n_row, n_x, n_zh, T * n_dp),
             out_shape=(
@@ -440,7 +423,7 @@
                 jax.ShapeDtypeStruct((own, width), f32),
             ),
             in_specs=[hbm] * 6,
-            out_specs=(anywhere,) * 5,
+            out_specs=(pl.BlockSpec(memory_space=pltpu.VMEM),) * 5,
             scratch_shapes=scratch,
             compiler_params=pltpu.CompilerParams(
                 collective_id=0, has_side_effects=True, vmem_limit_bytes=48 * 1024 * 1024

time: 44.2 us -> 44 us (level)
  no operation moved by 1% of the time
where the time goes in v5:
time: 44 us; the launch traced here: 43.9 us
  Pallas kernels  43.2 us (98%)
  between operations  0.64 us (1%)
    pallas_call x1, Pallas kernels, per_device(): pl.pallas_call(functools.partial(kernel, n_row, n_x, n_zh, T * n_dp), out...  42.2 us
    pallas_call x1, Pallas kernels, write_out(): pl.pallas_call(write_kernel, out_shape=tuple((jax.ShapeDtypeStruct(a.shap...  1.08 us

profile of v5, /device:TPU:1, one launch (start us, length us, event | category | flops | bytes accessed | tf_op | source)
XLA Modules:
  0.0 43.9 jit_solution(12671053128621040505)
XLA Ops:
  0.6 42.2 %shard_map.101 = (bf16[3,8,1792]{2,1,0:T(8,128)(2,1)S(1)}, bf16[3,8,512]{2,1,0:T(8,128)(2,1)S(1)}, bf16[64,1792]{1,0:T(8,128)(2,1)S(1)}, f32[64,1792]{1,0:T(8,128)S(1)}, f32[64,1792]{1,0:T(8,128)S(1)}) custom-call(bf16[192,512]{1,0:T(8,128)(2,1)} %x_ref.1, bf16[512,1792]{1,0:T(8,128)(2,1)} %w_ref.1, bf16[3,8,1792]{2,1,0:T(8,128)(2,1)} %bitcast.5, ...), custom_call_target="tpu_custom_call" | custom-call | tf_op jit(solution)/shard_map/pallas_call | solution.py:416
  42.8 1.1 %shard_map.102 = (bf16[24,1792]{1,0:T(8,128)(2,1)}, bf16[24,512]{1,0:T(8,128)(2,1)}, bf16[64,1792]{1,0:T(8,128)(2,1)}, f32[64,1792]{1,0:T(8,128)}, f32[64,1792]{1,0:T(8,128)}) custom-call(bf16[24,1792]{1,0:T(8,128)(2,1)S(1)} %bitcast.3, bf16[24,512]{1,0:T(8,128)(2,1)S(1)} %bitcast.4, bf16[64,1792]{1,0:T(8,128)(2,1)S(1)} %get-tuple-element.12.refs_2_, ...), custom_call_target="tpu_custom_call" | custom-call | tf_op jit(solution)/shard_map/pallas_call | solution.py:377
